TPU v7x, 32 devices: a whole 2x2x4 slice. The times are simulated.
32 devices in a mesh: lat: 16 (over z, y, x), field: 2 (over core).
Axes of the slice: x: 2, y: 2, z: 4, core: 2. Of those that a mesh axis runs over, the one named last changes fastest.
Arguments:
- fields_grid: bfloat16 [2, 64, 2, 48, 192], P('field', None, None, 'lat'), may hold values from -6 to 6
- basis: bfloat16 [128, 48, 96], P('lat'), may hold values from -0.875 to 0.875
- order_table: int32 [16, 8], replicated, may hold values from -1 to 95, as said below
- panel_modes: int32 [2, 64], replicated, may hold values from 0 to 95, as said below
Outputs:
- panel: bfloat16 [2, 128, 192, 128], P('field', 'lat')
Inputs may be any that keep to these rules, and one draw needn't show every extreme that they name: `order_table`: each order 0 to 95 stands in exactly one slot; every other slot holds -1; some group has all 8 slots filled. `panel_modes`: row 1 is never smaller than row 0 in the same column; degree 95 appears.
All inputs are finite; a program needn't handle non-finite values.
Results may differ from a plain program's by a relative error of at most 0.0082.
Values may be sent and summed in bfloat16 or wider, within the bound.
A program may use at most 64 MiB of HBM per device.

v0:
```python
import math
import jax
import jax.numpy as jnp
from jax import lax
from jax.sharding import PartitionSpec as P


def dft_table(orders, lon_count):
    valid_slot = orders >= 0
    safe_orders = jnp.maximum(orders, 0)
    products = lax.broadcasted_iota(jnp.int32, (lon_count, 1), 0) * safe_orders[None, :] % lon_count
    angles = products.astype(jnp.float32) * (2.0 * math.pi / lon_count)
    cosine = jnp.where(valid_slot[None, :], jnp.cos(angles), 0.0).astype(jnp.bfloat16)
    sine_table = jnp.where(valid_slot[None, :], -jnp.sin(angles), 0.0).astype(jnp.bfloat16)
    return jnp.stack([cosine, sine_table], axis=1)


def local(fields_grid, basis, order_table, panel_modes):
    grid_one = fields_grid[0]
    snap_count = grid_one.shape[0]
    pair_count = grid_one.shape[2]
    lon_count = grid_one.shape[3]
    slot_count = order_table.shape[1]
    deg_count = basis.shape[2]
    pair_total = basis.shape[1]
    mode_count = panel_modes.shape[1]
    orders = order_table.reshape(-1)
    slot_all = orders.shape[0]
    dft = dft_table(orders, lon_count)
    fourier = jnp.einsum("thjn,nrk->hkjrt", grid_one, dft, preferred_element_type=jnp.float32) * (
        1.0 / math.sqrt(lon_count)
    )
    fourier = fourier.reshape(2, slot_all, pair_count, 2 * snap_count)
    parity_parts = jnp.stack([fourier[0] + fourier[1], fourier[0] - fourier[1]]).astype(
        jnp.bfloat16
    )
    group_index = lax.axis_index("lat")
    my_orders = lax.dynamic_slice_in_dim(order_table, group_index, 1, 0)[0]
    my_odd = my_orders % 2 == 1
    basis_split = basis.reshape(slot_count, pair_total, deg_count // 2, 2)
    even_rows = basis_split[:, :, :, 0]
    odd_rows = basis_split[:, :, :, 1]
    degree = lax.broadcasted_iota(jnp.int32, (1, deg_count), 1)
    keep_mask = (degree >= my_orders[:, None]) & (my_orders >= 0)[:, None]
    received = lax.all_to_all(parity_parts, "lat", split_axis=1, concat_axis=2, tiled=True)
    first_parity = jnp.where(my_odd[:, None, None], received[1], received[0])
    second = jnp.where(my_odd[:, None, None], received[0], received[1])
    low_degrees = jnp.einsum(
        "sjh,sjc->shc", even_rows, first_parity, preferred_element_type=jnp.float32
    )
    high_degrees = jnp.einsum("sjh,sjc->shc", odd_rows, second, preferred_element_type=jnp.float32)
    joined = jnp.stack([low_degrees, high_degrees], axis=2).reshape(slot_count, deg_count, -1)
    coefficients = jnp.where(keep_mask[:, :, None], joined, 0.0).astype(jnp.bfloat16)
    mode_order = panel_modes[0]
    mode_degree = panel_modes[1]
    onehot = (my_orders[None, :] == mode_order[:, None]).astype(jnp.bfloat16)
    picked = jnp.take(coefficients, mode_degree, axis=1)
    local_values = jnp.einsum("ms,smc->mc", onehot, picked, preferred_element_type=jnp.float32)
    field_index = lax.axis_index("field")
    both_fields = jnp.stack(
        [
            jnp.where(field_index == 0, local_values, 0.0),
            jnp.where(field_index == 1, local_values, 0.0),
        ]
    )
    summed = lax.psum(both_fields, ("lat", "field"))
    other_field = jnp.where(field_index == 0, summed[1], summed[0]).astype(jnp.bfloat16)
    columns = other_field.astype(jnp.float32).reshape(mode_count * 2, snap_count)
    centered = (columns - jnp.mean(columns, axis=1, keepdims=True)).astype(jnp.bfloat16)
    coef_rows = coefficients.reshape(slot_count * deg_count * 2, snap_count)
    panel_values = lax.dot_general(
        coef_rows, centered, (((1,), (1,)), ((), ())), preferred_element_type=jnp.float32
    )
    panel_values = panel_values * (1.0 / (snap_count - 1))
    return panel_values.astype(jnp.bfloat16).reshape(1, slot_count, 2 * deg_count, 2 * mode_count)


def solution(mesh):
    placed = (P("field", None, None, "lat", None), P("lat", None, None), P(), P())
    return jax.shard_map(
        local, mesh=mesh, in_specs=placed, out_specs=P("field", "lat", None, None), check_vma=False
    )
```

profile of v0, /device:TPU:0, one launch (start us, length us, event | category | flops | bytes accessed | tf_op | source)
XLA Modules:
  0.0 63.5 jit_solution(17050038539362757233)
XLA Ops:
  0.0 0.8 %broadcast_compare_fusion = pred[16,8]{0,1:T(8,128)(4,1)S(1)} fusion(s32[16,8]{0,1:T(8,128)} %param.6), kind=kLoop, calls=%fused_computation.57 | loop fusion | flops 128 | bytes 640 | tf_op jit(solution)/shard_map/ge | solution.py:9
  0.8 0.0 copy-done.1
  0.8 0.1 copy.39
  0.9 0.1 ge.51
  1.0 0.1 copy.40
  1.0 0.1 max.11
  1.1 0.4 select_convert_fusion.1
  1.6 1.1 %fusion.1 = f32[2,128,3,2,64]{1,4,2,0,3:T(8,128)S(1)} fusion(bf16[64,2,3,192]{3,1,2,0:T(2,128)(2,1)} %bitcast.69, bf16[192,1,128]{2,0,1:T(8,128)(2,1)S(1)} %get-tuple-element.16, bf16[192,1,128]{2,0,1:T(8,128)(2,1)S(1)} %get-tuple-element.15), kind=kOutput, calls=%fused_computation.4 | convolution fusion | flops 38043648 | bytes 638976 | tf_op jit(solution)/shard_map/thjn,nrk->hkjrt/dot_general | solution.py:30
  2.8 0.8 %copy.44 = bf16[2,128,3,128]{3,0,2,1:T(2,128)(2,1)} copy(bf16[2,128,3,128]{1,3,2,0:T(8,128)(2,1)S(1)} %pad_maximum_fusion.1) | data formatting | bytes 393216 | tf_op jit(solution)/shard_map/stack | solution.py:34
  3.7 8.5 %all-to-all-start = ((bf16[2,128,3,128]{3,0,2,1:T(2,128)(2,1)}), bf16[2,128,3,128]{3,0,2,1:T(2,128)(2,1)S(1)}, u32[]{:S(2)}, u32[]{:S(2)}) async-start(bf16[2,128,3,128]{3,0,2,1:T(2,128)(2,1)} %copy.44), calls=%async_computation | async-start | bytes 393216 | tf_op jit(solution)/shard_map/all_to_all | solution.py:45
  12.1 0.0 copy-start.2
  12.2 0.7 %copy-done.2 = s32[2,64]{1,0:T(2,128)S(1)} copy-done((s32[2,64]{1,0:T(2,128)S(1)}, s32[2,64]{1,0:T(2,128)}, u32[]{:S(2)}) %copy-start.2) | copy-done | bytes 536
  12.8 0.2 dynamic-slice_reduce_fusion
  13.0 0.1 compare_bitcast_fusion
  13.2 0.2 copy.48
  13.4 7.4 %all-to-all-done = bf16[2,128,3,128]{3,0,2,1:T(2,128)(2,1)S(1)} async-done(((bf16[2,128,3,128]{3,0,2,1:T(2,128)(2,1)}), bf16[2,128,3,128]{3,0,2,1:T(2,128)(2,1)S(1)}, u32[]{:S(2)}, u32[]{:S(2)}) %all-to-all-start) | async-done | bytes 196640 | tf_op jit(solution)/shard_map/all_to_all | solution.py:45
  20.9 0.1 bitcast_select_fusion.2
  21.0 0.2 convolution_bitcast_fusion.1
  21.2 0.2 convolution_bitcast_fusion
  21.4 0.1 copy.53
  21.5 0.2 fusion.2
  21.7 0.6 gather_fusion
  22.3 0.3 fusion.5
  22.6 39.0 %psum.7 = bf16[2,64,128]{2,1,0:T(8,128)(2,1)S(1)} all-reduce(f32[2,64,128]{2,1,0:T(8,128)S(1)} %pad_maximum_fusion.2), channel_id=1, replica_groups=mesh['lat'=16,'field'=2] {'lat','field'}, use_global_device_ids=true, to_apply=%region_0.1 | all-reduce | flops 16384 | bytes 98304 | tf_op jit(solution)/shard_map/psum | solution.py:66
  61.6 0.1 reshape.345
  61.7 0.1 reduce_sum.9
  61.8 0.1 div.10
  62.0 0.1 sub.26
  62.1 0.1 sub.27
  62.2 0.1 convert_element_type.92
  62.3 0.2 convert_element_type.86
  62.5 1.0 %fusion = bf16[1536,128]{1,0:T(8,128)(2,1)} fusion(bf16[1536,64]{1,0:T(8,128)(2,1)S(1)} %convert_element_type.86, bf16[128,64]{1,0:T(8,128)(2,1)S(1)} %convert_element_type.92), kind=kOutput, calls=%fused_computation.2 | convolution fusion | flops 25559040 | bytes 606208 | tf_op jit(solution)/shard_map/dot_general | solution.py:71
  (26 shorter events, 0.3 us)
Async XLA Ops:
  0.0 0.8 %copy-start.1 = (s32[16,8]{0,1:T(8,128)S(1)}, s32[16,8]{0,1:T(8,128)}, u32[]{:S(2)}) copy-start(s32[16,8]{0,1:T(8,128)} %param.6) | copy-start | bytes 1540
  3.7 9.5 %copy-start = (bf16[8,48,96]{2,1,0:T(8,128)(2,1)S(1)}, bf16[8,48,96]{2,1,0:T(8,128)(2,1)}, u32[]{:S(2)}) copy-start(bf16[8,48,96]{2,1,0:T(8,128)(2,1)} %param.5) | copy-start | bytes 221188
  3.7 17.1 %all-to-all-start = ((bf16[2,128,3,128]{3,0,2,1:T(2,128)(2,1)}), bf16[2,128,3,128]{3,0,2,1:T(2,128)(2,1)S(1)}, u32[]{:S(2)}, u32[]{:S(2)}) async-start(bf16[2,128,3,128]{3,0,2,1:T(2,128)(2,1)} %copy.44), calls=%async_computation | async-start | bytes 393216 | tf_op jit(solution)/shard_map/all_to_all | solution.py:45
  12.1 0.7 %copy-start.2 = (s32[2,64]{1,0:T(2,128)S(1)}, s32[2,64]{1,0:T(2,128)}, u32[]{:S(2)}) copy-start(s32[2,64]{1,0:T(2,128)} %param.7) | copy-start | bytes 1540
where the time goes:
time: 63.9 us; the launch traced here: 63.5 us
  blocking collectives  39 us (61%)
  starting transfers between devices  8.47 us (13%)
  waiting for transfers between devices  7.41 us (12%)
  local copies, waits for them, and re-layouts  3.74 us (6%)
  matrix products  2.79 us (4%)
  other arithmetic  1.84 us (3%)
    psum x1, blocking collectives, local(): summed = lax.psum(both_fields, ('lat', 'field'))  39 us
    all_to_all x1, starting transfers between devices, local(): lax.all_to_all(parity_parts, 'lat', split_axis=1, concat_axis=2, tiled=True)  8.47 us
    all_to_all x1, waiting for transfers between devices, local(): lax.all_to_all(parity_parts, 'lat', split_axis=1, concat_axis=2, tiled=True)  7.41 us
  transfers between devices with their start and end apart: 1, of which 1 were waited for; matrix products, arithmetic and copies ran while one was open for 1% of the time, Pallas kernels for 0%

commit v1 on v0

--- a/solution.py
+++ b/solution.py
@@ -63,7 +63,7 @@
             jnp.where(field_index == 1, local_values, 0.0),
         ]
     )
-    summed = lax.psum(both_fields, ("lat", "field"))
+    summed = jnp.sum(lax.all_gather(both_fields, ("lat", "field")), axis=0)
     other_field = jnp.where(field_index == 0, summed[1], summed[0]).astype(jnp.bfloat16)
     columns = other_field.astype(jnp.float32).reshape(mode_count * 2, snap_count)
     centered = (columns - jnp.mean(columns, axis=1, keepdims=True)).astype(jnp.bfloat16)

time: 63.9 us -> 95 us (1.49)
  waiting for transfers between devices: 7.41 us -> 61.9 us
  blocking collectives: 39 us -> 0 us
  between operations: 0.28 us -> 13.7 us
  other arithmetic: 1.84 us -> 4.86 us
    all_gather x0 -> x1, waiting for transfers between devices: none -> 53.9 us  [local(): summed = jnp.sum(lax.all_gather(both_fields, ('lat', 'field')), axis=0)]
    psum x1 -> x0, blocking collectives: 39 us -> none  [local(): summed = lax.psum(both_fields, ('lat', 'field'))]
    reduce_sum x0 -> x1, other arithmetic: none -> 1.7 us  [local(): summed = jnp.sum(lax.all_gather(both_fields, ('lat', 'field')), axis=0)]
  transfers between devices with their start and end apart: 1 -> 2, of which waited for: 1 -> 2; matrix products, arithmetic and copies ran while one was open for 1% -> 1% of each run, Pallas kernels for 0% -> 0%
where the time goes in v1:
time: 95 us; the launch traced here: 94.7 us
  waiting for transfers between devices  61.9 us (65%)
  between operations  13.7 us (14%)
  starting transfers between devices  8.38 us (9%)
  other arithmetic  4.86 us (5%)
  local copies, waits for them, and re-layouts  3.08 us (3%)
  matrix products  2.79 us (3%)
    all_gather x1, waiting for transfers between devices, local(): summed = jnp.sum(lax.all_gather(both_fields, ('lat', 'field')), axis=0)  53.9 us
    all_to_all x1, starting transfers between devices, local(): lax.all_to_all(parity_parts, 'lat', split_axis=1, concat_axis=2, tiled=True)  8.34 us
    all_to_all x1, waiting for transfers between devices, local(): lax.all_to_all(parity_parts, 'lat', split_axis=1, concat_axis=2, tiled=True)  8 us
  transfers between devices with their start and end apart: 2, of which 2 were waited for; matrix products, arithmetic and copies ran while one was open for 1% of the time, Pallas kernels for 0%

profile of v1, /device:TPU:0, one launch (start us, length us, event | category | flops | bytes accessed | tf_op | source)
XLA Modules:
  0.0 94.7 jit_solution(6620204686136337275)
XLA Ops:
  6.5 0.8 broadcast_compare_fusion
  7.3 0.7 broadcast_maximum_fusion
  8.0 0.1 copy.39
  8.1 0.1 ge.51
  8.2 0.1 copy.40
  8.2 0.1 max.11
  8.3 0.4 select_convert_fusion.1
  8.8 1.1 %fusion.1 = f32[2,128,3,2,64]{1,4,2,0,3:T(8,128)S(1)} fusion(bf16[64,2,3,192]{3,1,2,0:T(2,128)(2,1)} %bitcast.71, bf16[192,1,128]{2,0,1:T(8,128)(2,1)S(1)} %get-tuple-element.16, bf16[192,1,128]{2,0,1:T(8,128)(2,1)S(1)} %get-tuple-element.15), kind=kOutput, calls=%fused_computation.4 | convolution fusion | flops 38043648 | bytes 638976 | tf_op jit(solution)/shard_map/thjn,nrk->hkjrt/dot_general | solution.py:30
  10.0 0.8 copy.44
  10.9 8.3 %all-to-all-start = ((bf16[2,128,3,128]{3,0,2,1:T(2,128)(2,1)}), bf16[2,128,3,128]{3,0,2,1:T(2,128)(2,1)S(1)}, u32[]{:S(2)}, u32[]{:S(2)}) async-start(bf16[2,128,3,128]{3,0,2,1:T(2,128)(2,1)} %copy.44), calls=%async_computation | async-start | bytes 393216 | tf_op jit(solution)/shard_map/all_to_all | solution.py:45
  19.3 0.2 dynamic-slice_reduce_fusion
  19.5 0.1 compare_bitcast_fusion
  19.7 0.2 copy.48
  19.9 8.0 %all-to-all-done = bf16[2,128,3,128]{3,0,2,1:T(2,128)(2,1)S(1)} async-done(((bf16[2,128,3,128]{3,0,2,1:T(2,128)(2,1)}), bf16[2,128,3,128]{3,0,2,1:T(2,128)(2,1)S(1)}, u32[]{:S(2)}, u32[]{:S(2)}) %all-to-all-start) | async-done | bytes 196640 | tf_op jit(solution)/shard_map/all_to_all | solution.py:45
  28.0 0.1 bitcast_select_fusion.2
  28.1 0.2 convolution_bitcast_fusion.1
  28.3 0.2 convolution_bitcast_fusion
  28.5 0.1 copy.53
  28.5 0.2 fusion.2
  28.7 0.6 gather_fusion
  29.4 0.3 fusion.5
  29.6 0.6 pad_maximum_fusion.2
  30.3 0.2 convert_element_type.86
  30.5 53.9 %all-gather.3.cloned.1.call-done = f32[64,64,128]{2,1,0:T(8,128)} async-done(((f32[2,64,128]{2,1,0:T(8,128)}), f32[64,64,128]{2,1,0:T(8,128)}) %all-gather.3.cloned.1.call-update) | async-done | bytes 2097168 | tf_op jit(solution)/shard_map/all_gather | solution.py:66
  84.4 1.7 %reduce_sum.18 = bf16[2,64,128]{2,1,0:T(8,128)(2,1)S(1)} reduce(f32[32,2,64,128]{3,2,1,0:T(8,128)} %bitcast.66, f32[]{:T(128)} %constant.60.clone.1), dimensions={0}, to_apply=%region_0.1 | reduce | flops 507904 | bytes 2129924 | tf_op jit(solution)/shard_map/reduce_sum | solution.py:66
  86.1 0.1 reshape.345
  86.2 0.1 reduce_sum.19
  86.3 0.1 div.10
  86.5 0.1 sub.26
  86.6 0.1 sub.27
  86.7 0.1 convert_element_type.92
  86.8 1.0 %fusion = bf16[1536,128]{1,0:T(8,128)(2,1)} fusion(bf16[1536,64]{1,0:T(8,128)(2,1)S(1)} %convert_element_type.86, bf16[128,64]{1,0:T(8,128)(2,1)S(1)} %convert_element_type.92), kind=kOutput, calls=%fused_computation.2 | convolution fusion | flops 25559040 | bytes 606208 | tf_op jit(solution)/shard_map/dot_general | solution.py:71
  (29 shorter events, 0.4 us)
Async XLA Ops:
  6.5 12.8 %copy-start.1 = (s32[16,8]{0,1:T(8,128)S(1)}, s32[16,8]{0,1:T(8,128)}, u32[]{:S(2)}) copy-start(s32[16,8]{0,1:T(8,128)} %param.6) | copy-start | bytes 1540
  6.5 12.7 %copy-start.2 = (s32[2,64]{1,0:T(2,128)S(1)}, s32[2,64]{1,0:T(2,128)}, u32[]{:S(2)}) copy-start(s32[2,64]{1,0:T(2,128)} %param.7) | copy-start | bytes 1540
  6.5 13.1 %copy-start = (bf16[8,48,96]{2,1,0:T(8,128)(2,1)S(1)}, bf16[8,48,96]{2,1,0:T(8,128)(2,1)}, u32[]{:S(2)}) copy-start(bf16[8,48,96]{2,1,0:T(8,128)(2,1)} %param.5) | copy-start | bytes 221188
  10.9 17.0 %all-to-all-start = ((bf16[2,128,3,128]{3,0,2,1:T(2,128)(2,1)}), bf16[2,128,3,128]{3,0,2,1:T(2,128)(2,1)S(1)}, u32[]{:S(2)}, u32[]{:S(2)}) async-start(bf16[2,128,3,128]{3,0,2,1:T(2,128)(2,1)} %copy.44), calls=%async_computation | async-start | bytes 393216 | tf_op jit(solution)/shard_map/all_to_all | solution.py:45
  19.2 65.2 %all-gather.3.cloned.1.call-start = ((), (), s32[]{:S(2)}) async-start(), calls=%async_computation.1 | async-start | bytes 2162688 | tf_op jit(solution)/shard_map/all_gather | solution.py:66
Sparse Core Ops, SparseCore 0:
  30.4 53.9 all-gather.2
